TPU v7x, 768 devices: a whole 4x8x12 slice. The times are simulated.
768 devices in a mesh: ctx: 32 (over y, z_lo), dp: 24 (over x, z_hi, core).
Axes of the slice: x: 4, y: 8, z: 12 (z_hi: 3, z_lo: 4; z = z_hi * 4 + z_lo), core: 2. Of those that a mesh axis runs over, the one named last changes fastest.
Arguments:
- queries: bfloat16 [24, 4096, 2048], P('dp', 'ctx'), may hold values from -110 to 110
- keys: bfloat16 [24, 4096, 512], P('dp', 'ctx'), may hold values from -4 to 4
- values: bfloat16 [24, 4096, 512], P('dp', 'ctx'), may hold values from -4 to 4
- grad_out: bfloat16 [24, 4096, 2048], P('dp', 'ctx'), may hold values from -12 to 12
- sinks: float32 [16], replicated, may hold values from 0 to 6
- doc_ids: int32 [24, 32], P('dp'), may hold values from 0 to 7, never falling along the last dimension, each value on 1 to 16 neighbouring positions
Outputs:
- grad_queries: bfloat16 [24, 4096, 2048], P('dp', 'ctx')
- grad_keys: bfloat16 [24, 4096, 512], P('dp', 'ctx')
- grad_values: bfloat16 [24, 4096, 512], P('dp', 'ctx')
- grad_sinks: float32 [16], replicated
All inputs are finite; a program needn't handle non-finite values.
Results may differ from a plain program's by a relative error of at most 0.017.
Values may be sent and summed in bfloat16 or wider, within the bound.
A program may use at most 32 MiB of HBM per device.

v0:
```python
import jax
import jax.numpy as jnp
from jax import lax
from jax.sharding import PartitionSpec as P

BLOCK = 128
WINDOW = 512


def passed_along(value, axis, steps):
    count = lax.axis_size(axis)
    initial, last = (max(0, -steps), min(count, count - steps))
    return lax.ppermute(value, axis, [(source, source + steps) for source in range(initial, last)])


def local(queries, keys, values, grad_out, sinks, doc_ids):
    row_count = queries.shape[1]
    head_count = sinks.shape[0]
    head_size = queries.shape[2] // head_count
    kv_count = keys.shape[2] // head_size
    group_size = head_count // kv_count
    reach_count = -(-WINDOW // row_count)
    key_count = (reach_count + 1) * row_count
    shard_index = lax.axis_index("ctx")
    score_scale = head_size ** (-0.5)
    own_kv = jnp.stack([keys[0], values[0]])
    remote = []
    for distance in range(1, reach_count + 1):
        remote.append(passed_along(own_kv, "ctx", distance))
    window_kv = jnp.concatenate(remote[::-1] + [own_kv], axis=1)
    key_rows = window_kv[0].reshape(key_count, kv_count, head_size)
    value_rows = window_kv[1].reshape(key_count, kv_count, head_size)
    own_blocks = row_count // BLOCK
    doc_row = doc_ids[0]
    padded_docs = jnp.concatenate([jnp.full((reach_count * own_blocks,), -1, jnp.int32), doc_row])
    query_docs = lax.dynamic_slice_in_dim(doc_row, shard_index * own_blocks, own_blocks)
    key_docs = lax.dynamic_slice_in_dim(padded_docs, shard_index * own_blocks, key_count // BLOCK)
    same_doc = jnp.broadcast_to(
        query_docs[:, None, None, None] == key_docs[None, None, :, None],
        (own_blocks, BLOCK, key_count // BLOCK, BLOCK),
    ).reshape(row_count, key_count)
    offsets = (
        reach_count * row_count
        + jnp.arange(row_count, dtype=jnp.int32)[:, None]
        - jnp.arange(key_count, dtype=jnp.int32)[None, :]
    )
    allowed = same_doc & (offsets >= 0) & (offsets < WINDOW)
    query_rows = queries[0].reshape(row_count, kv_count, group_size, head_size)
    cotangent = grad_out[0].reshape(row_count, kv_count, group_size, head_size)
    sink_grid = sinks.reshape(kv_count, group_size)
    query_parts, key_parts, value_parts, sink_parts = ([], [], [], [])
    for member in range(kv_count):
        q_part = query_rows[:, member]
        g_part = cotangent[:, member]
        k_part = key_rows[:, member]
        v_part = value_rows[:, member]
        sink_col = sink_grid[member][:, None]
        scores = (
            jnp.einsum("tgd,kd->gtk", q_part, k_part, preferred_element_type=jnp.float32)
            * score_scale
        )
        masked = jnp.where(allowed[None], scores, -jnp.inf)
        top_score = jnp.maximum(jnp.max(masked, axis=-1), sink_col)
        raised = jnp.exp(masked - top_score[..., None])
        sink_weight = jnp.exp(sink_col - top_score)
        summed = sink_weight + jnp.sum(raised, axis=-1)
        probs = (raised / summed[..., None]).astype(jnp.bfloat16)
        attended = jnp.einsum("gtk,kd->tgd", probs, v_part, preferred_element_type=jnp.float32)
        delta = jnp.transpose(jnp.sum(g_part.astype(jnp.float32) * attended, axis=-1))
        sink_parts.append(-jnp.sum(sink_weight / summed * delta, axis=-1))
        grad_probs = jnp.einsum("tgd,kd->gtk", g_part, v_part, preferred_element_type=jnp.float32)
        grad_scores = (probs.astype(jnp.float32) * (grad_probs - delta[..., None])).astype(
            jnp.bfloat16
        )
        query_parts.append(
            (
                jnp.einsum("gtk,kd->tgd", grad_scores, k_part, preferred_element_type=jnp.float32)
                * score_scale
            ).astype(jnp.bfloat16)
        )
        key_parts.append(
            jnp.einsum("gtk,tgd->kd", grad_scores, q_part, preferred_element_type=jnp.float32)
            * score_scale
        )
        value_parts.append(
            jnp.einsum("gtk,tgd->kd", probs, g_part, preferred_element_type=jnp.float32)
        )
    grad_queries = jnp.stack(query_parts, axis=1).reshape(1, row_count, head_count * head_size)
    kv_grads = jnp.stack([jnp.stack(key_parts, axis=1), jnp.stack(value_parts, axis=1)]).reshape(
        2, key_count, kv_count * head_size
    )

    def share_for(distance):
        return lax.slice_in_dim(
            kv_grads,
            (reach_count - distance) * row_count,
            (reach_count - distance + 1) * row_count,
            axis=1,
        )

    running = share_for(0)
    for distance in range(1, reach_count + 1):
        running = running + passed_along(share_for(distance), "ctx", -distance)
    grad_sinks = lax.psum(jnp.concatenate(sink_parts), ("ctx", "dp"))
    return (
        grad_queries,
        running[0][None].astype(jnp.bfloat16),
        running[1][None].astype(jnp.bfloat16),
        grad_sinks,
    )


def solution(mesh):
    in_specs = (
        P("dp", "ctx", None),
        P("dp", "ctx", None),
        P("dp", "ctx", None),
        P("dp", "ctx", None),
        P(),
        P("dp", None),
    )
    out_specs = (P("dp", "ctx", None), P("dp", "ctx", None), P("dp", "ctx", None), P())
    return jax.shard_map(local, mesh=mesh, in_specs=in_specs, out_specs=out_specs, check_vma=False)
```

profile of v0, /device:TPU:1, one launch (start us, length us, event | category | flops | bytes accessed | tf_op | source)
XLA Modules:
  0.0 227.9 jit_solution(10579460096681681635)
XLA Ops:
  0.6 1.1 copy.49
  1.7 1.0 copy.50
  3.5 4.8 %collective-permute-start.3 = (bf16[2,128,512]{1,2,0:T(8,128)(2,1)}, bf16[2,128,512]{1,2,0:T(8,128)(2,1)S(1)}, u32[]{:S(2)}, u32[]{:S(2)}) collective-permute-start(bf16[2,128,512]{1,2,0:T(8,128)(2,1)} %pad_maximum_fusion.4), channel_id=1, source_target_pairs={{0,24},{24,48},{48,72},{72,96},{96,120},{120,144},{144,168},{168,1... | collective-permute-start | bytes 786440 | tf_op jit(solution)/shard_map/ppermute | solution.py:13
  8.3 6.5 %collective-permute-start.2 = (bf16[2,128,512]{1,2,0:T(8,128)(2,1)}, bf16[2,128,512]{1,2,0:T(8,128)(2,1)}, u32[]{:S(2)}, u32[]{:S(2)}) collective-permute-start(bf16[2,128,512]{1,2,0:T(8,128)(2,1)} %pad_maximum_fusion.4), channel_id=1, source_target_pairs={{0,48},{24,72},{48,96},{72,120},{96,144},{120,168},{144,192},{168,... | collective-permute-start | bytes 786440 | tf_op jit(solution)/shard_map/ppermute | solution.py:13
  14.8 3.2 %collective-permute-start.1 = (bf16[2,128,512]{1,2,0:T(8,128)(2,1)}, bf16[2,128,512]{1,2,0:T(8,128)(2,1)}, u32[]{:S(2)}, u32[]{:S(2)}) collective-permute-start(bf16[2,128,512]{1,2,0:T(8,128)(2,1)} %pad_maximum_fusion.4), channel_id=1, source_target_pairs={{0,72},{24,96},{48,120},{72,144},{96,168},{120,192},{144,216},{168... | collective-permute-start | bytes 786440 | tf_op jit(solution)/shard_map/ppermute | solution.py:13
  18.0 3.2 %collective-permute-start = (bf16[2,128,512]{1,2,0:T(8,128)(2,1)}, bf16[2,128,512]{1,2,0:T(8,128)(2,1)}, u32[]{:S(2)}, u32[]{:S(2)}) collective-permute-start(bf16[2,128,512]{1,2,0:T(8,128)(2,1)} %pad_maximum_fusion.4), channel_id=1, source_target_pairs={{0,96},{24,120},{48,144},{72,168},{96,192},{120,216},{144,240},{16... | collective-permute-start | bytes 786440 | tf_op jit(solution)/shard_map/ppermute | solution.py:13
  21.3 1.2 constant_dynamic-slice_fusion
  22.5 1.4 dynamic-slice_compare_fusion
  25.4 10.3 %collective-permute-done = bf16[2,128,512]{1,2,0:T(8,128)(2,1)} collective-permute-done((bf16[2,128,512]{1,2,0:T(8,128)(2,1)}, bf16[2,128,512]{1,2,0:T(8,128)(2,1)}, u32[]{:S(2)}, u32[]{:S(2)}) %collective-permute-start) | collective-permute-done | bytes 262176 | tf_op jit(solution)/shard_map/ppermute | solution.py:13
  40.0 1.1 convolution_bitcast_fusion.4
  45.0 1.1 convolution_bitcast_fusion.5
  48.1 1.1 convolution_bitcast_fusion.6
  51.0 1.1 convolution_bitcast_fusion.7
  54.5 2.4 %pad_maximum_fusion.1 = f32[640,4,128]{0,2,1:T(8,128)} fusion(f32[640,1,128]{0,2,1:T(8,128)} %convolution_bitcast_fusion.4, f32[640,1,128]{0,2,1:T(8,128)} %convolution_bitcast_fusion.5, f32[640,1,128]{0,2,1:T(8,128)} %convolution_bitcast_fusion.6, f32[640,1,128]{0,2,1:T(8,128)} %convolution_bitcast_fusion.7), kind=kLoop, calls=%fused_computation.37 | loop fusion | flops 983040 | bytes 2621440 | tf_op jit(solution)/shard_map/stack | solution.py:89
  57.0 1.7 copy.106
  58.8 115.0 %psum.7 = f32[16]{0:T(128)} all-reduce(f32[16]{0:T(128)S(1)} %pad_maximum_fusion.5), channel_id=1, replica_groups=mesh['ctx'=32,'dp'=24] {'ctx','dp'}, use_global_device_ids=true, to_apply=%region_16.17 | all-reduce | flops 16 | bytes 128 | tf_op jit(solution)/shard_map/psum | solution.py:104
  173.8 1.3 fusion.55
  175.1 1.4 collective-permute-start.4
  176.5 1.3 collective-permute-start.5
  177.8 1.3 collective-permute-start.7
  179.1 1.4 collective-permute-start.6
  182.5 8.2 %collective-permute-done.4 = f32[2,128,512]{2,1,0:T(8,128)} collective-permute-done((f32[2,128,512]{2,1,0:T(8,128)}, f32[2,128,512]{2,1,0:T(8,128)}, u32[]{:S(2)}, u32[]{:S(2)}) %collective-permute-start.4) | collective-permute-done | bytes 524320 | tf_op jit(solution)/shard_map/ppermute | solution.py:13
  190.8 34.6 %collective-permute-done.5 = f32[2,128,512]{2,1,0:T(8,128)} collective-permute-done((f32[2,128,512]{2,1,0:T(8,128)}, f32[2,128,512]{2,1,0:T(8,128)}, u32[]{:S(2)}, u32[]{:S(2)}) %collective-permute-start.5) | collective-permute-done | bytes 524320 | tf_op jit(solution)/shard_map/ppermute | solution.py:13
  225.4 1.8 fusion.54
  (91 shorter events, 19.1 us)
Async XLA Ops:
  0.6 23.3 %copy-start.6 = (bf16[1,128,2048]{2,1,0:T(8,128)(2,1)S(1)}, bf16[1,128,2048]{2,1,0:T(8,128)(2,1)}, u32[]{:S(2)}) copy-start(bf16[1,128,2048]{2,1,0:T(8,128)(2,1)} %param.9) | copy-start | bytes 1572868
  2.8 21.7 %copy-start.9 = (f32[16]{0:T(128)S(1)}, f32[16]{0:T(128)}, u32[]{:S(2)}) copy-start(f32[16]{0:T(128)} %param.10) | copy-start | bytes 196
  2.8 21.8 %copy-start.7 = (bf16[1,128,2048]{2,1,0:T(8,128)(2,1)S(1)}, bf16[1,128,2048]{2,1,0:T(8,128)(2,1)}, u32[]{:S(2)}) copy-start(bf16[1,128,2048]{2,1,0:T(8,128)(2,1)} %param.6) | copy-start | bytes 1572868
  3.5 35.3 %collective-permute-start.3 = (bf16[2,128,512]{1,2,0:T(8,128)(2,1)}, bf16[2,128,512]{1,2,0:T(8,128)(2,1)S(1)}, u32[]{:S(2)}, u32[]{:S(2)}) collective-permute-start(bf16[2,128,512]{1,2,0:T(8,128)(2,1)} %pad_maximum_fusion.4), channel_id=1, source_target_pairs={{0,24},{24,48},{48,72},{72,96},{96,120},{120,144},{144,168},{168,1... | collective-permute-start | bytes 786440 | tf_op jit(solution)/shard_map/ppermute | solution.py:13
  8.3 29.4 %collective-permute-start.2 = (bf16[2,128,512]{1,2,0:T(8,128)(2,1)}, bf16[2,128,512]{1,2,0:T(8,128)(2,1)}, u32[]{:S(2)}, u32[]{:S(2)}) collective-permute-start(bf16[2,128,512]{1,2,0:T(8,128)(2,1)} %pad_maximum_fusion.4), channel_id=1, source_target_pairs={{0,48},{24,72},{48,96},{72,120},{96,144},{120,168},{144,192},{168,... | collective-permute-start | bytes 786440 | tf_op jit(solution)/shard_map/ppermute | solution.py:13
  14.8 21.9 %collective-permute-start.1 = (bf16[2,128,512]{1,2,0:T(8,128)(2,1)}, bf16[2,128,512]{1,2,0:T(8,128)(2,1)}, u32[]{:S(2)}, u32[]{:S(2)}) collective-permute-start(bf16[2,128,512]{1,2,0:T(8,128)(2,1)} %pad_maximum_fusion.4), channel_id=1, source_target_pairs={{0,72},{24,96},{48,120},{72,144},{96,168},{120,192},{144,216},{168... | collective-permute-start | bytes 786440 | tf_op jit(solution)/shard_map/ppermute | solution.py:13
  18.0 17.7 %collective-permute-start = (bf16[2,128,512]{1,2,0:T(8,128)(2,1)}, bf16[2,128,512]{1,2,0:T(8,128)(2,1)}, u32[]{:S(2)}, u32[]{:S(2)}) collective-permute-start(bf16[2,128,512]{1,2,0:T(8,128)(2,1)} %pad_maximum_fusion.4), channel_id=1, source_target_pairs={{0,96},{24,120},{48,144},{72,168},{96,192},{120,216},{144,240},{16... | collective-permute-start | bytes 786440 | tf_op jit(solution)/shard_map/ppermute | solution.py:13
  39.0 5.0 %copy-start.4 = (bf16[1,640,512]{1,2,0:T(8,128)(2,1)}, bf16[1,640,512]{1,2,0:T(8,128)(2,1)S(1)}, u32[]{:S(2)}) copy-start(bf16[1,640,512]{1,2,0:T(8,128)(2,1)S(1)} %get-tuple-element.17) | copy-start | bytes 1966084
  50.1 0.9 copy-start
  53.3 0.9 copy-start.2
  173.8 6.8 %copy-start.5 = (bf16[1,640,512]{1,2,0:T(8,128)(2,1)S(1)}, bf16[1,640,512]{1,2,0:T(8,128)(2,1)}, u32[]{:S(2)}) copy-start(bf16[1,640,512]{1,2,0:T(8,128)(2,1)} %copy-done.4) | copy-start | bytes 1966084
  173.8 7.1 %copy-start.1 = (bf16[4,128,640]{1,2,0:T(8,128)(2,1)S(1)}, bf16[4,128,640]{1,2,0:T(8,128)(2,1)}, u32[]{:S(2)}) copy-start(bf16[4,128,640]{1,2,0:T(8,128)(2,1)} %copy-done) | copy-start | bytes 1966084
  175.1 6.0 %copy-start.3 = (bf16[4,128,640]{1,2,0:T(8,128)(2,1)S(1)}, bf16[4,128,640]{1,2,0:T(8,128)(2,1)}, u32[]{:S(2)}) copy-start(bf16[4,128,640]{1,2,0:T(8,128)(2,1)} %copy-done.2) | copy-start | bytes 1966084
  175.1 15.7 %collective-permute-start.4 = (f32[2,128,512]{2,1,0:T(8,128)}, f32[2,128,512]{2,1,0:T(8,128)}, u32[]{:S(2)}, u32[]{:S(2)}) collective-permute-start(f32[2,128,512]{2,1,0:T(8,128)} %get-tuple-element.12), channel_id=1, source_target_pairs={{24,0},{48,24},{72,48},{96,72},{120,96},{144,120},{168,144},{192,1... | collective-permute-start | bytes 1572872 | tf_op jit(solution)/shard_map/ppermute | solution.py:13
  176.5 48.9 %collective-permute-start.5 = (f32[2,128,512]{2,1,0:T(8,128)}, f32[2,128,512]{2,1,0:T(8,128)}, u32[]{:S(2)}, u32[]{:S(2)}) collective-permute-start(f32[2,128,512]{2,1,0:T(8,128)} %get-tuple-element.13), channel_id=1, source_target_pairs={{48,0},{72,24},{96,48},{120,72},{144,96},{168,120},{192,144},{216,... | collective-permute-start | bytes 1572872 | tf_op jit(solution)/shard_map/ppermute | solution.py:13
  177.8 47.6 %collective-permute-start.7 = (f32[2,128,512]{2,1,0:T(8,128)}, f32[2,128,512]{2,1,0:T(8,128)}, u32[]{:S(2)}, u32[]{:S(2)}) collective-permute-start(f32[2,128,512]{2,1,0:T(8,128)} %get-tuple-element.14), channel_id=1, source_target_pairs={{96,0},{120,24},{144,48},{168,72},{192,96},{216,120},{240,144},{26... | collective-permute-start | bytes 1572872 | tf_op jit(solution)/shard_map/ppermute | solution.py:13
  179.1 2.3 %copy-start.8 = (bf16[128,1,4,128]{0,3,2,1:T(8,128)(2,1)S(1)}, bf16[128,1,4,128]{0,3,2,1:T(8,128)(2,1)}, u32[]{:S(2)}) copy-start(bf16[128,1,4,128]{0,3,2,1:T(8,128)(2,1)} %fusion.44) | copy-start | bytes 393220
  179.1 46.2 %collective-permute-start.6 = (f32[2,128,512]{2,1,0:T(8,128)}, f32[2,128,512]{2,1,0:T(8,128)}, u32[]{:S(2)}, u32[]{:S(2)}) collective-permute-start(f32[2,128,512]{2,1,0:T(8,128)} %get-tuple-element.15), channel_id=1, source_target_pairs={{72,0},{96,24},{120,48},{144,72},{168,96},{192,120},{216,144},{240... | collective-permute-start | bytes 1572872 | tf_op jit(solution)/shard_map/ppermute | solution.py:13
where the time goes:
time: 228 us
  blocking collectives  115 us (50%)
  waiting for transfers between devices  53.2 us (23%)
  starting transfers between devices  23.2 us (10%)
  matrix products  12.5 us (5%)
  local copies, waits for them, and re-layouts  12.1 us (5%)
  other arithmetic  10.8 us (5%)
    psum x1, blocking collectives, local(): grad_sinks = lax.psum(jnp.concatenate(sink_parts), ('ctx', 'dp'))  115 us
    ppermute x8, waiting for transfers between devices, passed_along(): lax.ppermute(value, axis, [(source, source + steps) for source in range(i...  53.2 us
    ppermute x8, starting transfers between devices, passed_along(): lax.ppermute(value, axis, [(source, source + steps) for source in range(i...  23.2 us
    unnamed x33, local copies, waits for them, and re-layouts  7.73 us
  transfers between devices with their start and end apart: 8, of which 3 were waited for; matrix products, arithmetic and copies ran while one was open for 4% of the time, Pallas kernels for 0%

commit v1 on v0

v1 whole, which is shorter than its diff:
```python
import functools

import jax
import jax.numpy as jnp
from jax import lax
from jax.experimental import pallas as pl
from jax.experimental.pallas import tpu as pltpu
from jax.sharding import PartitionSpec as P

MESH = pl.DeviceIdType.MESH
ROWS = 128
HEAD = 128
GROUP = 4
ROW_CHIPS = 4
SLOTS = 5
NEG = -1e30
LOG2E = 1.4426950408889634
PRE = 2


def dp_factors(count):
    if count == 24:
        return (("core", 2, 1), ("x", 4, 6), ("zh", 3, 2))
    return (("core", count, 1),)


def kernel(
    layout,
    q_hbm,
    k_hbm,
    v_hbm,
    g_hbm,
    sink_ref,
    doc_ref,
    dq_hbm,
    dk_ref,
    dv_ref,
    ds_ref,
    q_buf,
    g_buf,
    win,
    part,
    out_buf,
    back,
    dq_buf,
    *rest,
):
    chunks, ctx_count, stages = layout
    stage_bufs = rest[: len(stages)]
    stage_send = rest[len(stages) : 2 * len(stages)]
    stage_recv = rest[2 * len(stages) : 3 * len(stages)]
    load_sem, kv_sem, dq_sem, f_send, f_recv, b_send, b_recv = rest[3 * len(stages) :]
    y_count = ctx_count // ROW_CHIPS
    ctx = lax.axis_index("ctx")
    dp = lax.axis_index("dp")
    zl = ctx % ROW_CHIPS
    y = ctx // ROW_CHIPS

    def load_kv(c, which):
        source = k_hbm if which == 0 else v_hbm
        return pltpu.make_async_copy(
            source.at[0, :, pl.ds(c * HEAD, HEAD)], win.at[c, 0, which], kv_sem.at[c, which]
        )

    def load_rows(c, which):
        source, target = (q_hbm, q_buf) if which == 0 else (g_hbm, g_buf)
        return pltpu.make_async_copy(
            source.at[0, :, pl.ds(pl.multiple_of(c * GROUP * HEAD, GROUP * HEAD), GROUP * HEAD)],
            target.at[c],
            load_sem.at[c, which],
        )

    def store_dq(c):
        return pltpu.make_async_copy(
            dq_buf.at[c],
            dq_hbm.at[0, :, pl.ds(pl.multiple_of(c * GROUP * HEAD, GROUP * HEAD), GROUP * HEAD)],
            dq_sem.at[c],
        )

    def stage_info(s):
        axis, size, stride = stages[s]
        index = ctx if axis == "ctx" else dp
        return axis, size, stride, (index // stride) % size, index

    def partner(s, step):
        axis, size, stride, mine, index = stage_info(s)
        other = (mine + step) % size
        return other, {axis: index + (other - mine) * stride}

    for c in range(chunks):
        load_kv(c, 0).start()
        load_kv(c, 1).start()
    for c in range(chunks):
        load_rows(c, 0).start()
        load_rows(c, 1).start()

    barrier = pltpu.get_barrier_semaphore()
    total_partners = 0
    for s in range(len(stages)):
        for step in range(1, stages[s][1]):
            _, device = partner(s, step)
            pl.semaphore_signal(barrier, inc=1, device_id=device, device_id_type=MESH)
            total_partners += 1

    @pl.when(y == 0)
    def _():
        for d in range(1, SLOTS):

            @pl.when(zl < d)
            def _():
                win[:, d] = jnp.zeros((chunks, 2, ROWS, HEAD), jnp.bfloat16)

    for c in range(chunks):
        load_kv(c, 0).wait()
        load_kv(c, 1).wait()
    pl.semaphore_wait(barrier, total_partners)

    def forward(c, source, target, sem, step):
        return pltpu.make_async_remote_copy(
            src_ref=win.at[c, source],
            dst_ref=win.at[c, target],
            send_sem=f_send.at[c, sem],
            recv_sem=f_recv.at[c, target],
            device_id={"ctx": ctx + step},
            device_id_type=MESH,
        )

    def backward(c, source, target, step):
        return pltpu.make_async_remote_copy(
            src_ref=out_buf.at[c, source - 1],
            dst_ref=back.at[c, target],
            send_sem=b_send.at[c, source],
            recv_sem=b_recv.at[c, target],
            device_id={"ctx": ctx + step},
            device_id_type=MESH,
        )

    def send_own(c):
        @pl.when(zl < ROW_CHIPS - 1)
        def _():
            forward(c, 0, 1, 0, 1).start()

        @pl.when(y < y_count - 1)
        def _():
            forward(c, 0, 4, 5, ROW_CHIPS).start()

    def relay(c, d):
        @pl.when((zl >= d) | (y > 0))
        def _():
            forward(c, d, d, d, 0).wait_recv()

        if d < ROW_CHIPS:

            @pl.when((zl >= d) & (zl < ROW_CHIPS - 1))
            def _():
                forward(c, d, d + 1, d, 1).start()

        @pl.when((zl < d) & (zl > 0) & (y > 0))
        def _():
            forward(c, d, d - 1, d, -1).start()

    own_doc = doc_ref[0, ctx]
    penalties = []
    for d in range(SLOTS):
        same = (doc_ref[0, (ctx - d + ctx_count) % ctx_count] == own_doc) & (ctx >= d)
        penalties.append(jnp.where(same, 0.0, NEG))
    scale = HEAD ** (-0.5)

    def compute(c):
        load_rows(c, 0).wait()
        load_rows(c, 1).wait()
        q_rows = q_buf[c]
        g_rows = g_buf[c]
        split = lambda a: jnp.concatenate(
            [a[:, h * HEAD : (h + 1) * HEAD] for h in range(GROUP)], axis=0
        )
        q = split(q_rows)
        g = split(g_rows)
        k = win[c, :, 0].reshape(SLOTS * ROWS, HEAD)
        v = win[c, :, 1].reshape(SLOTS * ROWS, HEAD)
        key_pos = lax.broadcasted_iota(jnp.int32, (ROWS, ROWS), 0)
        query_pos = lax.broadcasted_iota(jnp.int32, (ROWS, ROWS), 1)
        near = jnp.where(key_pos <= query_pos, 0.0, NEG)
        far = jnp.where(key_pos > query_pos, penalties[4], NEG)
        biases = [near, penalties[1], penalties[2], penalties[3], far]
        dims = (((1,), (1,)), ((), ()))
        s_all = lax.dot_general(k, q, dims, preferred_element_type=jnp.float32)
        dp_all = lax.dot_general(v, g, dims, preferred_element_type=jnp.float32)
        p_cols, ds_cols = [], []
        for h in range(GROUP):
            cols = slice(h * ROWS, (h + 1) * ROWS)
            sink = sink_ref[c * GROUP + h] * LOG2E
            x = [
                s_all[d * ROWS : (d + 1) * ROWS, cols] * (scale * LOG2E) + biases[d]
                for d in range(SLOTS)
            ]
            joined = functools.reduce(jnp.maximum, x)
            top = jnp.maximum(jnp.max(joined, axis=0, keepdims=True), sink)
            e = [jnp.exp2(a - top) for a in x]
            sink_weight = jnp.exp2(sink - top)
            summed = sink_weight + jnp.sum(
                functools.reduce(jnp.add, e), axis=0, keepdims=True
            )
            inverse = 1.0 / summed
            p = [(a * inverse).astype(jnp.bfloat16) for a in e]
            wide = [a.astype(jnp.float32) for a in p]
            dp_h = [dp_all[d * ROWS : (d + 1) * ROWS, cols] for d in range(SLOTS)]
            delta = jnp.sum(
                functools.reduce(jnp.add, [a * b for a, b in zip(wide, dp_h)]),
                axis=0,
                keepdims=True,
            )
            ds = [(a * (b - delta)).astype(jnp.bfloat16) for a, b in zip(wide, dp_h)]
            p_cols.append(jnp.concatenate(p, axis=0))
            ds_cols.append(jnp.concatenate(ds, axis=0))
            stage_bufs[0][stage_info(0)[3], pl.ds(c * GROUP + h, 1), :] = -(
                sink_weight * inverse * delta
            )
        p_all = jnp.concatenate(p_cols, axis=1)
        ds_all = jnp.concatenate(ds_cols, axis=1)
        dv = jnp.dot(p_all, g, preferred_element_type=jnp.float32)
        dk = jnp.dot(ds_all, q, preferred_element_type=jnp.float32) * scale
        for d in range(SLOTS):
            part[c, d, 0] = dk[d * ROWS : (d + 1) * ROWS]
            part[c, d, 1] = dv[d * ROWS : (d + 1) * ROWS]

        def query_grads():
            dq_t = jnp.dot(k.T, ds_all, preferred_element_type=jnp.float32) * scale
            for h in range(GROUP):
                dq_buf[c, :, h * HEAD : (h + 1) * HEAD] = jnp.transpose(
                    dq_t[:, h * ROWS : (h + 1) * ROWS]
                ).astype(jnp.bfloat16)
            store_dq(c).start()

        return query_grads

    def pass_back(c, d, received, target, step):
        value = part[c, d]
        if received:
            backward(c, d, d, step).wait_recv()
            value = value + back[c, d].astype(jnp.float32)
        out_buf[c, d - 1] = value.astype(jnp.bfloat16)
        backward(c, d, target, step).start()

    def wave(w, c):
        @pl.when(zl == ROW_CHIPS - 1 - w)
        def _():
            for d in range(ROW_CHIPS - 1 - w, 0, -1):
                pass_back(c, d, w > 0, d - 1, -1)

        @pl.when((zl == w) & (y > 0))
        def _():
            for d in range(w + 1, SLOTS):
                if d < ROW_CHIPS:
                    pass_back(c, d, w > 0, d + 1, 1)
                else:
                    pass_back(c, d, w > 0, 5, -ROW_CHIPS)

    def stage_start(s):
        _, size, _, mine, _ = stage_info(s)
        for step in range(1, size):
            _, device = partner(s, step)
            pltpu.make_async_remote_copy(
                src_ref=stage_bufs[s].at[mine],
                dst_ref=stage_bufs[s].at[mine],
                send_sem=stage_send[s].at[step],
                recv_sem=stage_recv[s].at[mine],
                device_id=device,
                device_id_type=MESH,
            ).start()

    def stage_copy(s, step):
        _, size, _, mine, _ = stage_info(s)
        other, device = partner(s, step)
        return pltpu.make_async_remote_copy(
            src_ref=stage_bufs[s].at[mine],
            dst_ref=stage_bufs[s].at[other],
            send_sem=stage_send[s].at[step],
            recv_sem=stage_recv[s].at[other],
            device_id=device,
            device_id_type=MESH,
        )

    def stage_finish(s):
        size = stages[s][1]
        for step in range(1, size):
            stage_copy(s, step).wait_recv()
        total = stage_bufs[s][0]
        for i in range(1, size):
            total = total + stage_bufs[s][i]
        if s + 1 < len(stages):
            stage_bufs[s + 1][stage_info(s + 1)[3]] = total
            stage_start(s + 1)
        else:
            ds_ref[...] = total

    for c in range(min(PRE, chunks)):
        send_own(c)

    def step_body(t, carry):
        @pl.when(t + PRE < chunks)
        def _():
            send_own(t + PRE)

        for d in (4, 1, 3, 2):
            relay(t, d)
        query_grads = compute(t)
        wave(0, t)
        query_grads()
        for w in range(1, ROW_CHIPS):

            @pl.when(t >= w)
            def _():
                wave(w, t - w)

        return carry

    lax.fori_loop(0, chunks, step_body, 0)
    stage_start(0)
    for t in range(chunks, chunks + ROW_CHIPS - 1):
        for w in range(1, ROW_CHIPS):
            if 0 <= t - w < chunks:
                wave(w, t - w)
        if t - chunks < len(stages):
            stage_finish(t - chunks)
    for s in range(ROW_CHIPS - 1, len(stages) - 1):
        stage_finish(s)

    for c in range(chunks):

        @pl.when(zl < ROW_CHIPS - 1)
        def _():
            backward(c, 1, 0, 1).wait_recv()
            part[c, 0] += back[c, 0].astype(jnp.float32)

        @pl.when(y < y_count - 1)
        def _():
            backward(c, 1, 5, ROW_CHIPS).wait_recv()
            part[c, 0] += back[c, 5].astype(jnp.float32)

        dk_ref[0, :, c * HEAD : (c + 1) * HEAD] = part[c, 0, 0].astype(jnp.bfloat16)
        dv_ref[0, :, c * HEAD : (c + 1) * HEAD] = part[c, 0, 1].astype(jnp.bfloat16)

    if len(stages) > ROW_CHIPS - 1:
        stage_finish(len(stages) - 1)
    for c in range(chunks):
        store_dq(c).wait()

        @pl.when(zl < ROW_CHIPS - 1)
        def _():
            forward(c, 0, 1, 0, 1).wait_send()

        @pl.when(y < y_count - 1)
        def _():
            forward(c, 0, 4, 5, ROW_CHIPS).wait_send()

        for d in range(1, SLOTS):
            goes_right = (zl >= d) & (zl < ROW_CHIPS - 1)
            goes_left = (zl < d) & (zl > 0) & (y > 0)

            @pl.when(goes_right | goes_left)
            def _():
                forward(c, d, d, d, 1).wait_send()

            @pl.when((zl >= d) | (y > 0))
            def _():
                backward(c, d, d, 1).wait_send()

    for s in range(len(stages)):
        for step in range(1, stages[s][1]):
            stage_copy(s, step).wait_send()


def local(layout, queries, keys, values, grad_out, sinks, doc_ids):
    chunks, ctx_count, stages = layout
    rows, width = queries.shape[1:]
    heads = sinks.shape[0]
    bf16, f32 = jnp.bfloat16, jnp.float32
    anywhere = pl.BlockSpec(memory_space=pl.ANY)
    scalars = pl.BlockSpec(memory_space=pltpu.SMEM)
    vmem = pl.BlockSpec(memory_space=pltpu.VMEM)
    dma = pltpu.SemaphoreType.DMA
    grad_q, grad_k, grad_v, grad_s = pl.pallas_call(
        functools.partial(kernel, layout),
        out_shape=(
            jax.ShapeDtypeStruct(queries.shape, bf16),
            jax.ShapeDtypeStruct(keys.shape, bf16),
            jax.ShapeDtypeStruct(values.shape, bf16),
            jax.ShapeDtypeStruct((heads, ROWS), f32),
        ),
        in_specs=[anywhere] * 4 + [scalars] * 2,
        out_specs=(anywhere, vmem, vmem, vmem),
        scratch_shapes=[
            pltpu.VMEM((chunks, rows, GROUP * HEAD), bf16),
            pltpu.VMEM((chunks, rows, GROUP * HEAD), bf16),
            pltpu.VMEM((chunks, SLOTS, 2, ROWS, HEAD), bf16),
            pltpu.VMEM((chunks, SLOTS, 2, ROWS, HEAD), f32),
            pltpu.VMEM((chunks, SLOTS - 1, 2, ROWS, HEAD), bf16),
            pltpu.VMEM((chunks, SLOTS + 1, 2, ROWS, HEAD), bf16),
            pltpu.VMEM((chunks, rows, GROUP * HEAD), bf16),
        ]
        + [pltpu.VMEM((size, heads, ROWS), f32) for _, size, _ in stages]
        + [dma((size,)) for _, size, _ in stages] * 2
        + [
            dma((chunks, 2)),
            dma((chunks, 2)),
            dma((chunks,)),
            dma((chunks, 6)),
            dma((chunks, 6)),
            dma((chunks, 6)),
            dma((chunks, 6)),
        ],
        compiler_params=pltpu.CompilerParams(
            collective_id=0, has_side_effects=True, vmem_limit_bytes=67043328
        ),
    )(queries, keys, values, grad_out, sinks, doc_ids)
    return grad_q, grad_k, grad_v, jnp.sum(grad_s, axis=1)


def solution(mesh):
    ctx_count = mesh.shape["ctx"]
    stages = tuple(("dp", size, stride) for _, size, stride in dp_factors(mesh.shape["dp"]))
    stages += (("ctx", ROW_CHIPS, 1), ("ctx", ctx_count // ROW_CHIPS, ROW_CHIPS))
    layout = (4, ctx_count, stages)
    split = P("dp", "ctx", None)
    return jax.shard_map(
        functools.partial(local, layout),
        mesh=mesh,
        in_specs=(split, split, split, split, P(), P("dp", None)),
        out_specs=(split, split, split, P()),
        check_vma=False,
    )
```

time: 228 us -> 94.3 us (0.41)
  the two profiles are of different devices: /device:TPU:1 before, /device:TPU:8 now
where the time goes in v1:
time: 94.3 us; the launch traced here: 94.1 us
  Pallas kernels  88.6 us (94%)
  local copies, waits for them, and re-layouts  3.52 us (4%)
  other arithmetic  1.32 us (1%)
    pallas_call x1, Pallas kernels, local(): pl.pallas_call(functools.partial(kernel, layout), out_shape=(jax.ShapeDty...  88.6 us
    unnamed x7, local copies, waits for them, and re-layouts  3.52 us

profile of v1, /device:TPU:8, one launch (start us, length us, event | category | flops | bytes accessed | tf_op | source)
XLA Modules:
  0.0 94.1 jit_solution(1153268049201913780)
XLA Ops:
  0.6 88.6 %shard_map.93 = (bf16[1,128,2048]{2,1,0:T(8,128)(2,1)}, bf16[1,128,512]{2,1,0:T(8,128)(2,1)}, bf16[1,128,512]{2,1,0:T(8,128)(2,1)}, f32[16,128]{1,0:T(8,128)}) custom-call(bf16[1,128,2048]{2,1,0:T(8,128)(2,1)} %q_hbm.1, bf16[1,128,512]{2,1,0:T(8,128)(2,1)} %k_hbm.1, bf16[1,128,512]{2,1,0:T(8,128)(2,1)} %v_hbm.1, bf16[1,128,2048]{2,1,0:T(8,128)(2,1)} %g_hbm.1, ...), custom_call_target="tpu_custom_call" | custom-call | tf_op jit(solution)/shard_map/pallas_call | solution.py:383
  89.2 1.3 %reduce_sum.9 = f32[16]{0:T(128)} reduce(f32[16,128]{1,0:T(8,128)} %get-tuple-element.11, f32[]{:T(128)} %constant.0.clone.1), dimensions={1}, to_apply=%region_0.0 | reduce | flops 2032 | bytes 8260 | tf_op jit(solution)/shard_map/reduce_sum | solution.py:417
  90.5 0.0 copy-start.1
  90.5 1.9 %copy.13 = bf16[1,128,2048]{2,1,0:T(8,128)(2,1)} copy(bf16[1,128,2048]{2,1,0:T(8,128)(2,1)} %get-tuple-element.16) | data formatting | bytes 1048576
  92.5 0.0 copy-done.1
  92.5 0.0 copy-start
  92.5 0.7 copy.14
  93.1 0.3 copy-done
  93.4 0.7 copy.15
Async XLA Ops:
  90.5 1.9 %copy-start.1 = (bf16[1,128,512]{2,1,0:T(8,128)(2,1)S(1)}, bf16[1,128,512]{2,1,0:T(8,128)(2,1)}, u32[]{:S(2)}) copy-start(bf16[1,128,512]{2,1,0:T(8,128)(2,1)} %get-tuple-element.17) | copy-start | bytes 393220
  92.5 1.0 %copy-start = (bf16[1,128,512]{2,1,0:T(8,128)(2,1)S(1)}, bf16[1,128,512]{2,1,0:T(8,128)(2,1)}, u32[]{:S(2)}) copy-start(bf16[1,128,512]{2,1,0:T(8,128)(2,1)} %get-tuple-element.18) | copy-start | bytes 393220

commit v2 on v1

--- a/solution.py
+++ b/solution.py
@@ -15,13 +15,26 @@
 SLOTS = 5
 NEG = -1e30
 LOG2E = 1.4426950408889634
-PRE = 2
-
-
-def dp_factors(count):
-    if count == 24:
-        return (("core", 2, 1), ("x", 4, 6), ("zh", 3, 2))
-    return (("core", count, 1),)
+PRE = 4
+LAG = 3
+DIRECT = 1
+PIECES = 4
+
+
+def reduction_stages(ctx_count, dp_count):
+    row = ("ctx", ROW_CHIPS, 1)
+    column = ("ctx", ctx_count // ROW_CHIPS, ROW_CHIPS)
+    if dp_count == 24:
+        core, x, z_hi = ("dp", 2, 1), ("dp", 4, 6), ("dp", 3, 2)
+        return ((core, x), (z_hi, row), (column,))
+    return ((("dp", dp_count, 1),), (row,), (column,))
+
+
+def members(stage):
+    count = 1
+    for _, size, _ in stage:
+        count *= size
+    return count
 
 
 def kernel(
@@ -43,6 +56,7 @@
     out_buf,
     back,
     dq_buf,
+    sink_rows,
     *rest,
 ):
     chunks, ctx_count, stages = layout
@@ -51,6 +65,7 @@
     stage_recv = rest[2 * len(stages) : 3 * len(stages)]
     load_sem, kv_sem, dq_sem, f_send, f_recv, b_send, b_recv = rest[3 * len(stages) :]
     y_count = ctx_count // ROW_CHIPS
+    chained = chunks - DIRECT
     ctx = lax.axis_index("ctx")
     dp = lax.axis_index("dp")
     zl = ctx % ROW_CHIPS
@@ -77,15 +92,23 @@
             dq_sem.at[c],
         )
 
-    def stage_info(s):
-        axis, size, stride = stages[s]
-        index = ctx if axis == "ctx" else dp
-        return axis, size, stride, (index // stride) % size, index
+    where = {"ctx": ctx, "dp": dp}
+
+    def place(s):
+        total = 0
+        for axis, size, stride in stages[s]:
+            total = total * size + (where[axis] // stride) % size
+        return total
 
     def partner(s, step):
-        axis, size, stride, mine, index = stage_info(s)
-        other = (mine + step) % size
-        return other, {axis: index + (other - mine) * stride}
+        other = (place(s) + step) % members(stages[s])
+        device, rest_of = {}, other
+        for axis, size, stride in reversed(stages[s]):
+            mine = (where[axis] // stride) % size
+            move = (rest_of % size - mine) * stride
+            device[axis] = device.get(axis, where[axis]) + move
+            rest_of = rest_of // size
+        return other, device
 
     for c in range(chunks):
         load_kv(c, 0).start()
@@ -97,10 +120,14 @@
     barrier = pltpu.get_barrier_semaphore()
     total_partners = 0
     for s in range(len(stages)):
-        for step in range(1, stages[s][1]):
+        for step in range(1, members(stages[s])):
             _, device = partner(s, step)
             pl.semaphore_signal(barrier, inc=1, device_id=device, device_id_type=MESH)
             total_partners += 1
+    for step in (1, 2, 3, -1, -2, -3):
+        near = {"ctx": (ctx + step + ctx_count) % ctx_count}
+        pl.semaphore_signal(barrier, inc=1, device_id=near, device_id_type=MESH)
+        total_partners += 1
 
     @pl.when(y == 0)
     def _():
@@ -144,10 +171,14 @@
         def _():
             forward(c, 0, 4, 5, ROW_CHIPS).start()
 
+    def passes_on(d):
+        leftward = (zl < d) & (zl > 0) & (y > 0)
+        return leftward if d == 4 else ((zl >= d) & (zl < ROW_CHIPS - 1)) | leftward
+
     def relay(c, d):
-        @pl.when((zl >= d) | (y > 0))
-        def _():
-            forward(c, d, d, d, 0).wait_recv()
+        @pl.when(passes_on(d))
+        def _():
+            forward(c, d, d, d, 1).wait_recv()
 
         if d < ROW_CHIPS:
 
@@ -158,6 +189,13 @@
         @pl.when((zl < d) & (zl > 0) & (y > 0))
         def _():
             forward(c, d, d - 1, d, -1).start()
+
+    def arrive(c):
+        for d in (4, 1, 3, 2):
+
+            @pl.when(((zl >= d) | (y > 0)) & jnp.logical_not(passes_on(d)))
+            def _():
+                forward(c, d, d, d, 1).wait_recv()
 
     own_doc = doc_ref[0, ctx]
     penalties = []
@@ -213,9 +251,7 @@
             ds = [(a * (b - delta)).astype(jnp.bfloat16) for a, b in zip(wide, dp_h)]
             p_cols.append(jnp.concatenate(p, axis=0))
             ds_cols.append(jnp.concatenate(ds, axis=0))
-            stage_bufs[0][stage_info(0)[3], pl.ds(c * GROUP + h, 1), :] = -(
-                sink_weight * inverse * delta
-            )
+            sink_rows[pl.ds(c * GROUP + h, 1), :] = -(sink_weight * inverse * delta)
         p_all = jnp.concatenate(p_cols, axis=1)
         ds_all = jnp.concatenate(ds_cols, axis=1)
         dv = jnp.dot(p_all, g, preferred_element_type=jnp.float32)
@@ -256,87 +292,117 @@
                 else:
                     pass_back(c, d, w > 0, 5, -ROW_CHIPS)
 
-    def stage_start(s):
-        _, size, _, mine, _ = stage_info(s)
-        for step in range(1, size):
-            _, device = partner(s, step)
-            pltpu.make_async_remote_copy(
-                src_ref=stage_bufs[s].at[mine],
-                dst_ref=stage_bufs[s].at[mine],
-                send_sem=stage_send[s].at[step],
-                recv_sem=stage_recv[s].at[mine],
-                device_id=device,
-                device_id_type=MESH,
-            ).start()
-
-    def stage_copy(s, step):
-        _, size, _, mine, _ = stage_info(s)
+    def direct(c):
+        for d in (3, 2, 1, 4):
+
+            @pl.when(ctx >= d)
+            def _():
+                out_buf[c, d - 1] = part[c, d].astype(jnp.bfloat16)
+                backward(c, d, d, -d).start()
+
+    def stage_copy(s, step, outgoing):
+        mine = place(s)
         other, device = partner(s, step)
+        slot = mine if outgoing else other
         return pltpu.make_async_remote_copy(
             src_ref=stage_bufs[s].at[mine],
-            dst_ref=stage_bufs[s].at[other],
+            dst_ref=stage_bufs[s].at[slot],
             send_sem=stage_send[s].at[step],
-            recv_sem=stage_recv[s].at[other],
+            recv_sem=stage_recv[s].at[slot],
             device_id=device,
             device_id_type=MESH,
         )
 
+    def stage_start(s, value):
+        stage_bufs[s][place(s)] = value
+        for step in range(1, members(stages[s])):
+            stage_copy(s, step, True).start()
+
+    def sinks_start():
+        heads = sink_rows.shape[0]
+        head = lax.broadcasted_iota(jnp.int32, (heads, ROWS), 0)
+        lane = lax.broadcasted_iota(jnp.int32, (heads, ROWS), 1)
+        sums = jnp.sum(sink_rows[...], axis=1, keepdims=True)
+        stage_start(0, jnp.sum(jnp.where(head == lane, sums, 0.0), axis=0, keepdims=True))
+
     def stage_finish(s):
-        size = stages[s][1]
+        size = members(stages[s])
         for step in range(1, size):
-            stage_copy(s, step).wait_recv()
+            stage_copy(s, step, False).wait_recv()
         total = stage_bufs[s][0]
         for i in range(1, size):
             total = total + stage_bufs[s][i]
         if s + 1 < len(stages):
-            stage_bufs[s + 1][stage_info(s + 1)[3]] = total
-            stage_start(s + 1)
+            stage_start(s + 1, total)
         else:
             ds_ref[...] = total
 
     for c in range(min(PRE, chunks)):
         send_own(c)
 
-    def step_body(t, carry):
-        @pl.when(t + PRE < chunks)
-        def _():
+    def relays(t):
+        for c, d in ((t, 4), (t, 1), (t - 1, 3), (t - 2, 2)):
+            if isinstance(t, int):
+                if 0 <= c < chunks:
+                    relay(c, d)
+            else:
+
+                @pl.when(c < chunks)
+                def _():
+                    relay(c, d)
+
+    for t in range(LAG):
+        relays(t)
+        if t + PRE < chunks:
             send_own(t + PRE)
 
-        for d in (4, 1, 3, 2):
-            relay(t, d)
-        query_grads = compute(t)
-        wave(0, t)
+    def step_body(c, carry):
+        relays(c + LAG)
+        arrive(c)
+        query_grads = compute(c)
+
+        @pl.when(c == chunks - 1)
+        def _():
+            sinks_start()
+
+        @pl.when(c < chained)
+        def _():
+            wave(0, c)
+
+        @pl.when(c >= chained)
+        def _():
+            direct(c)
+
         query_grads()
         for w in range(1, ROW_CHIPS):
 
-            @pl.when(t >= w)
-            def _():
-                wave(w, t - w)
+            @pl.when((c >= w) & (c - w < chained))
+            def _():
+                wave(w, c - w)
 
         return carry
 
     lax.fori_loop(0, chunks, step_body, 0)
-    stage_start(0)
     for t in range(chunks, chunks + ROW_CHIPS - 1):
-        for w in range(1, ROW_CHIPS):
-            if 0 <= t - w < chunks:
-                wave(w, t - w)
         if t - chunks < len(stages):
             stage_finish(t - chunks)
+        for w in range(1, ROW_CHIPS):
+            if 0 <= t - w < chained:
+                wave(w, t - w)
     for s in range(ROW_CHIPS - 1, len(stages) - 1):
         stage_finish(s)
 
     for c in range(chunks):
-
-        @pl.when(zl < ROW_CHIPS - 1)
-        def _():
-            backward(c, 1, 0, 1).wait_recv()
-            part[c, 0] += back[c, 0].astype(jnp.float32)
-
-        @pl.when(y < y_count - 1)
-        def _():
-            backward(c, 1, 5, ROW_CHIPS).wait_recv()
-            part[c, 0] += back[c, 5].astype(jnp.float32)
+        if c < chained:
+            sources = [(0, zl < ROW_CHIPS - 1), (5, y < y_count - 1)]
+        else:
+            sources = [(d, ctx + d < ctx_count) for d in range(1, SLOTS)]
+        for slot, exists in sources:
+
+            @pl.when(exists)
+            def _():
+                backward(c, 1, slot, 1).wait_recv()
+                part[c, 0] += back[c, slot].astype(jnp.float32)
 
         dk_ref[0, :, c * HEAD : (c + 1) * HEAD] = part[c, 0, 0].astype(jnp.bfloat16)
         dv_ref[0, :, c * HEAD : (c + 1) * HEAD] = part[c, 0, 1].astype(jnp.bfloat16)
@@ -367,8 +433,28 @@
                 backward(c, d, d, 1).wait_send()
 
     for s in range(len(stages)):
-        for step in range(1, stages[s][1]):
-            stage_copy(s, step).wait_send()
+        for step in range(1, members(stages[s])):
+            stage_copy(s, step, True).wait_send()
+
+
+def hand_over(q_in, k_in, v_in, s_ref, q_out, k_out, v_out, s_out, *rest):
+    buffers, arrived, stored = rest[:3], rest[3:6], rest[6:]
+    arrays = ((q_in, q_out), (k_in, k_out), (v_in, v_out))
+    loads, stores = [], []
+    for (source, target), buffer, full, empty in zip(arrays, buffers, arrived, stored):
+        count, rows = buffer.shape[:2]
+        for i in range(count):
+            part = pl.ds(i * rows, rows)
+            loads.append(pltpu.make_async_copy(source.at[0, part], buffer.at[i], full.at[i]))
+            stores.append(pltpu.make_async_copy(buffer.at[i], target.at[0, part], empty.at[i]))
+    for load in loads:
+        load.start()
+    s_out[...] = s_ref[0, : s_out.shape[0]]
+    for load, store in zip(loads, stores):
+        load.wait()
+        store.start()
+    for store in stores:
+        store.wait()
 
 
 def local(layout, queries, keys, values, grad_out, sinks, doc_ids):
@@ -386,7 +472,7 @@
             jax.ShapeDtypeStruct(queries.shape, bf16),
             jax.ShapeDtypeStruct(keys.shape, bf16),
             jax.ShapeDtypeStruct(values.shape, bf16),
-            jax.ShapeDtypeStruct((heads, ROWS), f32),
+            jax.ShapeDtypeStruct((1, ROWS), f32),
         ),
         in_specs=[anywhere] * 4 + [scalars] * 2,
         out_specs=(anywhere, vmem, vmem, vmem),
@@ -398,9 +484,10 @@
             pltpu.VMEM((chunks, SLOTS - 1, 2, ROWS, HEAD), bf16),
             pltpu.VMEM((chunks, SLOTS + 1, 2, ROWS, HEAD), bf16),
             pltpu.VMEM((chunks, rows, GROUP * HEAD), bf16),
+            pltpu.VMEM((heads, ROWS), f32),
         ]
-        + [pltpu.VMEM((size, heads, ROWS), f32) for _, size, _ in stages]
-        + [dma((size,)) for _, size, _ in stages] * 2
+        + [pltpu.VMEM((members(stage), 1, ROWS), f32) for stage in stages]
+        + [dma((members(stage),)) for stage in stages] * 2
         + [
             dma((chunks, 2)),
             dma((chunks, 2)),
@@ -414,13 +501,26 @@
             collective_id=0, has_side_effects=True, vmem_limit_bytes=67043328
         ),
     )(queries, keys, values, grad_out, sinks, doc_ids)
-    return grad_q, grad_k, grad_v, jnp.sum(grad_s, axis=1)
+    sizes = [(PIECES, rows // PIECES, width)] + [(1, rows, keys.shape[2])] * 2
+    return pl.pallas_call(
+        hand_over,
+        out_shape=(
+            jax.ShapeDtypeStruct(queries.shape, bf16),
+            jax.ShapeDtypeStruct(keys.shape, bf16),
+            jax.ShapeDtypeStruct(values.shape, bf16),
+            jax.ShapeDtypeStruct((heads,), f32),
+        ),
+        in_specs=[anywhere] * 3 + [vmem],
+        out_specs=(anywhere, anywhere, anywhere, vmem),
+        scratch_shapes=[pltpu.VMEM(size, bf16) for size in sizes]
+        + [dma((size[0],)) for size in sizes] * 2,
+        compiler_params=pltpu.CompilerParams(vmem_limit_bytes=67043328),
+    )(grad_q, grad_k, grad_v, grad_s)
 
 
 def solution(mesh):
     ctx_count = mesh.shape["ctx"]
-    stages = tuple(("dp", size, stride) for _, size, stride in dp_factors(mesh.shape["dp"]))
-    stages += (("ctx", ROW_CHIPS, 1), ("ctx", ctx_count // ROW_CHIPS, ROW_CHIPS))
+    stages = reduction_stages(ctx_count, mesh.shape["dp"])
     layout = (4, ctx_count, stages)
     split = P("dp", "ctx", None)
     return jax.shard_map(

time: 94.3 us -> 69.2 us (0.73)
  Pallas kernels: 88.6 us -> 68.3 us
  local copies, waits for them, and re-layouts: 3.52 us -> 0 us
  other arithmetic: 1.32 us -> 0 us
    pallas_call x1, Pallas kernels: 88.6 us -> 65.3 us  [local(): pl.pallas_call(functools.partial(kernel, layout), out_shape=(jax.ShapeDty...]
    unnamed x7 -> x0, local copies, waits for them, and re-layouts: 3.52 us -> none
    pallas_call x0 -> x1, Pallas kernels: none -> 3.05 us  [local(): pl.pallas_call(hand_over, out_shape=(jax.ShapeDtypeStruct(queries.shape,...]
    reduce_sum x1 -> x0, other arithmetic: 1.32 us -> none  [local(): return (grad_q, grad_k, grad_v, jnp.sum(grad_s, axis=1))]
where the time goes in v2:
time: 69.2 us; the launch traced here: 69 us
  Pallas kernels  68.3 us (99%)
    pallas_call x1, Pallas kernels, local(): pl.pallas_call(functools.partial(kernel, layout), out_shape=(jax.ShapeDty...  65.3 us
    pallas_call x1, Pallas kernels, local(): pl.pallas_call(hand_over, out_shape=(jax.ShapeDtypeStruct(queries.shape,...  3.05 us

profile of v2, /device:TPU:8, one launch (start us, length us, event | category | flops | bytes accessed | tf_op | source)
XLA Modules:
  0.0 69.0 jit_solution(8059117462256156430)
XLA Ops:
  0.6 65.3 %shard_map.93 = (bf16[1,128,2048]{2,1,0:T(8,128)(2,1)}, bf16[1,128,512]{2,1,0:T(8,128)(2,1)}, bf16[1,128,512]{2,1,0:T(8,128)(2,1)}, f32[1,128]{1,0:T(1,128)}) custom-call(bf16[1,128,2048]{2,1,0:T(8,128)(2,1)} %q_hbm.1, bf16[1,128,512]{2,1,0:T(8,128)(2,1)} %k_hbm.1, bf16[1,128,512]{2,1,0:T(8,128)(2,1)} %v_hbm.1, bf16[1,128,2048]{2,1,0:T(8,128)(2,1)} %g_hbm.1, ...), custom_call_target="tpu_custom_call" | custom-call | tf_op jit(solution)/shard_map/pallas_call | solution.py:469
  65.9 3.1 %shard_map.94 = (bf16[1,128,2048]{2,1,0:T(8,128)(2,1)}, bf16[1,128,512]{2,1,0:T(8,128)(2,1)}, bf16[1,128,512]{2,1,0:T(8,128)(2,1)}, f32[16]{0:T(128)}) custom-call(bf16[1,128,2048]{2,1,0:T(8,128)(2,1)} %get-tuple-element.8.q_in, bf16[1,128,512]{2,1,0:T(8,128)(2,1)} %get-tuple-element.9.k_in, bf16[1,128,512]{2,1,0:T(8,128)(2,1)} %get-tuple-element.10.v_in, ...), custom_call_target="tpu_custom_call" | custom-call | tf_op jit(solution)/shard_map/pallas_call | solution.py:505

commit v3 on v2

--- a/solution.py
+++ b/solution.py
@@ -18,7 +18,6 @@
 PRE = 4
 LAG = 3
 DIRECT = 1
-PIECES = 4
 
 
 def reduction_stages(ctx_count, dp_count):
@@ -437,35 +436,31 @@
             stage_copy(s, step, True).wait_send()
 
 
-def hand_over(q_in, k_in, v_in, s_ref, q_out, k_out, v_out, s_out, *rest):
-    buffers, arrived, stored = rest[:3], rest[3:6], rest[6:]
-    arrays = ((q_in, q_out), (k_in, k_out), (v_in, v_out))
-    loads, stores = [], []
-    for (source, target), buffer, full, empty in zip(arrays, buffers, arrived, stored):
-        count, rows = buffer.shape[:2]
-        for i in range(count):
-            part = pl.ds(i * rows, rows)
-            loads.append(pltpu.make_async_copy(source.at[0, part], buffer.at[i], full.at[i]))
-            stores.append(pltpu.make_async_copy(buffer.at[i], target.at[0, part], empty.at[i]))
-    for load in loads:
-        load.start()
+def hand_over(q_in, k_in, v_in, s_ref, q_out, k_out, v_out, s_out, stored):
+    copies = [
+        pltpu.make_async_copy(source, target, stored.at[i])
+        for i, (source, target) in enumerate(((q_in, q_out), (k_in, k_out), (v_in, v_out)))
+    ]
+    for copy in copies:
+        copy.start()
     s_out[...] = s_ref[0, : s_out.shape[0]]
-    for load, store in zip(loads, stores):
-        load.wait()
-        store.start()
-    for store in stores:
-        store.wait()
+    for copy in copies:
+        copy.wait()
 
 
 def local(layout, queries, keys, values, grad_out, sinks, doc_ids):
     chunks, ctx_count, stages = layout
-    rows, width = queries.shape[1:]
+    rows = queries.shape[1]
     heads = sinks.shape[0]
     bf16, f32 = jnp.bfloat16, jnp.float32
     anywhere = pl.BlockSpec(memory_space=pl.ANY)
     scalars = pl.BlockSpec(memory_space=pltpu.SMEM)
     vmem = pl.BlockSpec(memory_space=pltpu.VMEM)
     dma = pltpu.SemaphoreType.DMA
+    operands = [
+        pltpu.with_memory_space_constraint(a, pltpu.HBM)
+        for a in (queries, keys, values, grad_out, sinks, doc_ids)
+    ]
     grad_q, grad_k, grad_v, grad_s = pl.pallas_call(
         functools.partial(kernel, layout),
         out_shape=(
@@ -498,10 +493,9 @@
             dma((chunks, 6)),
         ],
         compiler_params=pltpu.CompilerParams(
-            collective_id=0, has_side_effects=True, vmem_limit_bytes=67043328
+            collective_id=0, has_side_effects=True, vmem_limit_bytes=24 * 1024 * 1024
         ),
-    )(queries, keys, values, grad_out, sinks, doc_ids)
-    sizes = [(PIECES, rows // PIECES, width)] + [(1, rows, keys.shape[2])] * 2
+    )(*operands)
     return pl.pallas_call(
         hand_over,
         out_shape=(
@@ -512,9 +506,8 @@
         ),
         in_specs=[anywhere] * 3 + [vmem],
         out_specs=(anywhere, anywhere, anywhere, vmem),
-        scratch_shapes=[pltpu.VMEM(size, bf16) for size in sizes]
-        + [dma((size[0],)) for size in sizes] * 2,
-        compiler_params=pltpu.CompilerParams(vmem_limit_bytes=67043328),
+        scratch_shapes=[dma((3,))],
+        compiler_params=pltpu.CompilerParams(vmem_limit_bytes=4 * 1024 * 1024),
     )(grad_q, grad_k, grad_v, grad_s)
 
 

time: 69.2 us -> 66.8 us (0.965)
  Pallas kernels: 68.3 us -> 66 us
    pallas_call x1, Pallas kernels: 3.05 us -> 1.41 us  [local(): pl.pallas_call(hand_over, out_shape=(jax.ShapeDtypeStruct(queries.shape,...]
    pallas_call x1, Pallas kernels: 65.3 us -> 64.6 us  [local(): pl.pallas_call(functools.partial(kernel, layout), out_shape=(jax.ShapeDty...]
where the time goes in v3:
time: 66.8 us; the launch traced here: 66.6 us
  Pallas kernels  66 us (99%)
    pallas_call x1, Pallas kernels, local(): pl.pallas_call(functools.partial(kernel, layout), out_shape=(jax.ShapeDty...  64.6 us
    pallas_call x1, Pallas kernels, local(): pl.pallas_call(hand_over, out_shape=(jax.ShapeDtypeStruct(queries.shape,...  1.41 us

profile of v3, /device:TPU:8, one launch (start us, length us, event | category | flops | bytes accessed | tf_op | source)
XLA Modules:
  0.0 66.6 jit_solution(14635218337663128642)
XLA Ops:
  0.6 64.6 %shard_map.93 = (bf16[1,128,2048]{2,1,0:T(8,128)(2,1)S(1)}, bf16[1,128,512]{2,1,0:T(8,128)(2,1)S(1)}, bf16[1,128,512]{2,1,0:T(8,128)(2,1)S(1)}, f32[1,128]{1,0:T(1,128)S(1)}) custom-call(bf16[1,128,2048]{2,1,0:T(8,128)(2,1)} %q_hbm.1, bf16[1,128,512]{2,1,0:T(8,128)(2,1)} %k_hbm.1, bf16[1,128,512]{2,1,0:T(8,128)(2,1)} %v_hbm.1, bf16[1,128,2048]{2,1,0:T(8,128)(2,1)} %g_hbm.1, ...), custom_call_target="tpu_custom_call" | custom-call | tf_op jit(solution)/shard_map/pallas_call | solution.py:464
  65.2 1.4 %shard_map.94 = (bf16[1,128,2048]{2,1,0:T(8,128)(2,1)}, bf16[1,128,512]{2,1,0:T(8,128)(2,1)}, bf16[1,128,512]{2,1,0:T(8,128)(2,1)}, f32[16]{0:T(128)}) custom-call(bf16[1,128,2048]{2,1,0:T(8,128)(2,1)S(1)} %get-tuple-element.8.q_in, bf16[1,128,512]{2,1,0:T(8,128)(2,1)S(1)} %get-tuple-element.9.k_in, bf16[1,128,512]{2,1,0:T(8,128)(2,1)S(1)} %get-tuple-element.10.v_in, ...), custom_call_target="tpu_custom_call" | custom-call | tf_op jit(solution)/shard_map/pallas_call | solution.py:499
